TPU v7x, 32 devices: a whole 2x2x4 slice. The times are simulated.
32 devices in a mesh: cells: 8 (over y, x, core), vecs: 4 (over z).
Axes of the slice: x: 2, y: 2, z: 4, core: 2. Of those that a mesh axis runs over, the one named last changes fastest.
Arguments:
- vectors: float32 [64, 8, 64, 128], P(None, 'cells', 'vecs'), may hold values from -120 to 120
- potential: float32 [64, 8, 128], P(None, 'cells'), may hold values from -0.5 to 0.5
- hopping: float32 [27, 64, 64], replicated, may hold values from -0.07 to 0.07
- center: float32 [1], replicated, may hold values from -0.3 to 0.3
Outputs:
- filtered: float32 [64, 8, 64, 128], P(None, 'cells', 'vecs')
All inputs are finite; a program needn't handle non-finite values.
Results may differ from a plain program's by a relative error of at most 0.0003.
Values sent between devices are 32-bit elements; how exact they have to be, the bound alone decides.
A program may use at most 128 MiB of HBM per device.

v0:
```python
import math

import jax
import jax.numpy as jnp
from jax import lax
from jax.sharding import PartitionSpec as P

NVEC = 64
NY = 16
STEPS = 4
NZ = 8


HIGH = lax.Precision.HIGHEST


def with_halo(x, sides, width):
    for axis, dim in sides:
        peers, length = (lax.axis_size(axis), x.shape[dim])
        up = [(i, (i + 1) % peers) for i in range(peers)]
        down = [(j, i) for i, j in up]
        last = lax.slice_in_dim(x, length - width, length, axis=dim)
        initial = lax.slice_in_dim(x, 0, width, axis=dim)
        before = lax.ppermute(last, axis, up)
        after = lax.ppermute(initial, axis, down)
        x = jnp.concatenate([before, x, after], axis=dim)
    return x


def symmetric_blocks(hopping):
    return 0.5 * (hopping + jnp.transpose(hopping[::-1], (0, 2, 1)))


def apply_lattice(field_in, potential, center, blocks):
    orbits, width_x, bundle, merged = field_in.shape
    padded = with_halo(field_in, (("cells", 1),), 1)
    grid_view = padded.reshape(orbits, width_x + 2, bundle, NY, NZ)
    running = (potential - center[0])[:, :, None, :] * field_in
    for inner in range(9):
        shift_y = inner // 3 - 1
        shift_z = inner % 3 - 1
        shifted = jnp.roll(grid_view, (-shift_y, -shift_z), axis=(3, 4)).reshape(
            orbits, width_x + 2, bundle, merged
        )
        for offset in range(3):
            source = shifted[:, offset : offset + width_x].reshape(orbits, -1)
            product = jnp.dot(
                blocks[9 * offset + inner],
                source,
                precision=HIGH,
                preferred_element_type=jnp.float32,
            )
            running = running + product.reshape(orbits, width_x, bundle, merged)
    return running


def inner_rows(left, right):
    return lax.dot_general(
        left,
        right,
        (((0, 1, 3), (0, 1, 3)), ((), ())),
        precision=HIGH,
        preferred_element_type=jnp.float32,
    )


def shards(vectors, potential, hopping, center):
    blocks = symmetric_blocks(hopping)
    previous = vectors
    current = apply_lattice(vectors, potential, center, blocks)
    for step in range(STEPS - 1):
        following = 2.0 * apply_lattice(current, potential, center, blocks) - previous
        previous, current = (current, following)
    total_cells = current.shape[1] * lax.axis_size("cells") * current.shape[3]
    factor = math.sqrt(float(total_cells))
    by_cells = lax.all_to_all(current, "vecs", split_axis=3, concat_axis=2, tiled=True)
    gram_matrix = lax.psum(inner_rows(by_cells, by_cells), ("cells", "vecs"))
    frobenius = jnp.sqrt(jnp.sum(gram_matrix * gram_matrix))
    mixing = (1.5 * jnp.eye(NVEC, dtype=jnp.float32) - 0.5 * gram_matrix / frobenius) / jnp.sqrt(
        frobenius
    )
    mixed = jnp.einsum("oxuc,uv->oxvc", by_cells, mixing, precision=HIGH) * factor
    return lax.all_to_all(mixed, "vecs", split_axis=2, concat_axis=3, tiled=True)


def solution(mesh):
    placed = (P(None, "cells", "vecs", None), P(None, "cells", None), P(), P())
    return jax.shard_map(
        shards,
        mesh=mesh,
        in_specs=placed,
        out_specs=P(None, "cells", "vecs", None),
        check_vma=False,
    )
```

profile of v0, /device:TPU:0, one launch (start us, length us, event | category | flops | bytes accessed | tf_op | source)
XLA Modules:
  0.0 634.2 jit_solution(11029724212112709233)
XLA Ops:
  0.0 3.4 collective-permute-start.1
  10.7 6.4 %collective-permute-done = f32[64,1,16,128]{3,2,1,0:T(8,128)} collective-permute-done((f32[64,1,16,128]{3,2,1,0:T(8,128)}, f32[64,1,16,128]{3,2,1,0:T(8,128)}, u32[]{:S(2)}, u32[]{:S(2)}) %collective-permute-start) | collective-permute-done | bytes 524320 | tf_op jit(solution)/shard_map/ppermute | solution.py:24
  26.5 3.5 fusion.18
  30.0 5.5 fusion.19
  40.6 3.2 maximum_bitcast_fusion.3
  55.0 3.1 fusion.431
  68.2 3.1 fusion.432
  81.2 3.1 fusion.424
  106.3 2.6 maximum_bitcast_fusion.6
  147.0 5.2 fusion.44
  155.5 9.8 %collective-permute-done.3 = f32[64,1,16,128]{3,0,2,1:T(8,128)S(1)} collective-permute-done((f32[64,1,16,128]{3,0,2,1:T(8,128)S(1)}, f32[64,1,16,128]{3,0,2,1:T(8,128)S(1)}, u32[]{:S(2)}, u32[]{:S(2)}) %collective-permute-start.3) | collective-permute-done | bytes 524320 | tf_op jit(solution)/shard_map/ppermute | solution.py:25
  178.9 3.4 fusion.13
  182.3 3.5 fusion.16
  185.8 3.4 fusion.418
  202.1 3.1 fusion.420
  277.5 4.8 fusion.71
  286.9 8.7 %collective-permute-done.5 = f32[64,1,16,128]{3,0,2,1:T(8,128)S(1)} collective-permute-done((f32[64,1,16,128]{3,0,2,1:T(8,128)S(1)}, f32[64,1,16,128]{3,0,2,1:T(8,128)S(1)}, u32[]{:S(2)}, u32[]{:S(2)}) %collective-permute-start.5) | collective-permute-done | bytes 524320 | tf_op jit(solution)/shard_map/ppermute | solution.py:25
  309.5 3.4 fusion.7
  312.9 3.5 fusion.10
  316.4 3.4 fusion.406
  332.6 3.1 fusion.408
  408.2 4.8 fusion.100
  417.5 8.7 %collective-permute-done.7 = f32[64,1,16,128]{3,0,2,1:T(8,128)S(1)} collective-permute-done((f32[64,1,16,128]{3,0,2,1:T(8,128)S(1)}, f32[64,1,16,128]{3,0,2,1:T(8,128)S(1)}, u32[]{:S(2)}, u32[]{:S(2)}) %collective-permute-start.7) | collective-permute-done | bytes 524320 | tf_op jit(solution)/shard_map/ppermute | solution.py:25
  439.8 3.4 fusion.1
  443.2 3.5 fusion.4
  446.7 3.4 fusion.394
  462.9 3.1 fusion.396
  538.5 4.8 fusion.129
  545.4 16.3 %all_to_all.33 = f32[4,1,32768]{2,1,0:T(1,128)S(1)} all-to-all(f32[4,1,32768]{2,1,0:T(1,128)S(1)} %reshape.1488), channel_id=1, replica_groups=mesh['cells'=8,'vecs'=4] {'vecs'}, dimensions={0} | all-to-all | bytes 1048576 | tf_op jit(solution)/shard_map/all_to_all | solution.py:76
  567.9 39.4 %psum.7 = f32[64,64]{1,0:T(8,128)S(1)} all-reduce(f32[64,64]{1,0:T(8,128)S(1)} %convolution_bitcast_fusion.108), channel_id=1, replica_groups=mesh['cells'=8,'vecs'=4] {'cells','vecs'}, use_global_device_ids=true, to_apply=%region_0.1 | all-reduce | flops 4096 | bytes 32768 | tf_op jit(solution)/shard_map/psum | solution.py:77
  608.5 3.1 fusion.24
  612.9 17.1 %all_to_all.34 = f32[4,1,32768]{2,1,0:T(1,128)S(1)} all-to-all(f32[4,1,32768]{2,1,0:T(1,128)S(1)} %reshape.1490), channel_id=1, replica_groups=mesh['cells'=8,'vecs'=4] {'vecs'}, dimensions={0} | all-to-all | bytes 1048576 | tf_op jit(solution)/shard_map/all_to_all | solution.py:83
  (494 shorter events, 433.8 us)
Async XLA Ops:
  0.0 9.2 %copy-start.10 = (f32[64,1,16,128]{3,2,1,0:T(8,128)S(1)}, f32[64,1,16,128]{3,2,1,0:T(8,128)}, u32[]{:S(2)}) copy-start(f32[64,1,16,128]{3,2,1,0:T(8,128)} %param.4) | copy-start | bytes 1572868
  0.0 7.8 %copy-start.14 = (f32[27,64,64]{2,1,0:T(8,128)S(1)}, f32[27,64,64]{2,1,0:T(8,128)}, u32[]{:S(2)}) copy-start(f32[27,64,64]{2,1,0:T(8,128)} %param.6) | copy-start | bytes 1327108
  0.0 18.5 %collective-permute-start.1 = (f32[64,1,16,128]{3,2,1,0:T(8,128)}, f32[64,1,16,128]{3,2,1,0:T(8,128)}, u32[]{:S(2)}, u32[]{:S(2)}) collective-permute-start(f32[64,1,16,128]{3,2,1,0:T(8,128)} %param.4), channel_id=1, source_target_pairs={{4,0},{8,4},{12,8},{16,12},{20,16},{24,20},{28,24},{0,28},{5,1},{9... | collective-permute-start | bytes 1572872 | tf_op jit(solution)/shard_map/ppermute | solution.py:25
  3.4 13.7 %collective-permute-start = (f32[64,1,16,128]{3,2,1,0:T(8,128)}, f32[64,1,16,128]{3,2,1,0:T(8,128)}, u32[]{:S(2)}, u32[]{:S(2)}) collective-permute-start(f32[64,1,16,128]{3,2,1,0:T(8,128)} %param.4), channel_id=1, source_target_pairs={{0,4},{4,8},{8,12},{12,16},{16,20},{20,24},{24,28},{28,0},{1,5},{5... | collective-permute-start | bytes 1572872 | tf_op jit(solution)/shard_map/ppermute | solution.py:24
  4.8 5.9 copy-start.85
  9.1 144.9 %copy-start = (f32[27,64,64]{2,1,0:T(8,128)}, f32[27,64,64]{2,1,0:T(8,128)S(1)}, u32[]{:S(2)}) copy-start(f32[27,64,64]{2,1,0:T(8,128)S(1)} %fusion.139) | copy-start | bytes 1327108
  147.0 5.3 copy-start.18
  147.0 5.3 copy-start.36
  147.0 5.3 copy-start.37
  147.0 5.3 copy-start.38
  147.0 5.3 copy-start.48
  147.0 5.3 copy-start.49
  147.0 5.3 copy-start.50
  153.1 14.2 %copy-start.7 = (f32[64,1,16,128]{3,0,2,1:T(8,128)}, f32[64,1,16,128]{3,0,2,1:T(8,128)S(1)}, u32[]{:S(2)}) copy-start(f32[64,1,16,128]{3,0,2,1:T(8,128)S(1)} %fusion.51) | copy-start | bytes 1572868
  153.1 12.2 %collective-permute-start.3 = (f32[64,1,16,128]{3,0,2,1:T(8,128)S(1)}, f32[64,1,16,128]{3,0,2,1:T(8,128)S(1)}, u32[]{:S(2)}, u32[]{:S(2)}) collective-permute-start(f32[64,1,16,128]{3,0,2,1:T(8,128)S(1)} %fusion.51), channel_id=1, source_target_pairs={{4,0},{8,4},{12,8},{16,12},{20,16},{24,20},{28,24},{0,28},{5,1},{9... | collective-permute-start | bytes 1572872 | tf_op jit(solution)/shard_map/ppermute | solution.py:25
  153.2 14.1 %collective-permute-start.2 = (f32[64,1,16,128]{3,0,2,1:T(8,128)S(1)}, f32[64,1,16,128]{3,0,2,1:T(8,128)S(1)}, u32[]{:S(2)}, u32[]{:S(2)}) collective-permute-start(f32[64,1,16,128]{3,0,2,1:T(8,128)S(1)} %fusion.51), channel_id=1, source_target_pairs={{0,4},{4,8},{8,12},{12,16},{16,20},{20,24},{24,28},{28,0},{1,5},{5... | collective-permute-start | bytes 1572872 | tf_op jit(solution)/shard_map/ppermute | solution.py:24
  185.8 6.0 copy-start.54
  268.6 8.8 %copy-start.8 = (f32[64,1,16,128]{3,0,2,1:T(8,128)S(1)}, f32[64,1,16,128]{3,0,2,1:T(8,128)}, u32[]{:S(2)}) copy-start(f32[64,1,16,128]{3,0,2,1:T(8,128)} %copy-done.7) | copy-start | bytes 1572868
  283.4 14.3 %copy-start.4 = (f32[64,1,16,128]{3,0,2,1:T(8,128)}, f32[64,1,16,128]{3,0,2,1:T(8,128)S(1)}, u32[]{:S(2)}) copy-start(f32[64,1,16,128]{3,0,2,1:T(8,128)S(1)} %fusion.80) | copy-start | bytes 1572868
  283.4 12.2 %collective-permute-start.5 = (f32[64,1,16,128]{3,0,2,1:T(8,128)S(1)}, f32[64,1,16,128]{3,0,2,1:T(8,128)S(1)}, u32[]{:S(2)}, u32[]{:S(2)}) collective-permute-start(f32[64,1,16,128]{3,0,2,1:T(8,128)S(1)} %fusion.80), channel_id=1, source_target_pairs={{4,0},{8,4},{12,8},{16,12},{20,16},{24,20},{28,24},{0,28},{5,1},{9... | collective-permute-start | bytes 1572872 | tf_op jit(solution)/shard_map/ppermute | solution.py:25
  285.1 12.6 %collective-permute-start.4 = (f32[64,1,16,128]{3,0,2,1:T(8,128)S(1)}, f32[64,1,16,128]{3,0,2,1:T(8,128)S(1)}, u32[]{:S(2)}, u32[]{:S(2)}) collective-permute-start(f32[64,1,16,128]{3,0,2,1:T(8,128)S(1)} %fusion.80), channel_id=1, source_target_pairs={{0,4},{4,8},{8,12},{12,16},{16,20},{20,24},{24,28},{28,0},{1,5},{5... | collective-permute-start | bytes 1572872 | tf_op jit(solution)/shard_map/ppermute | solution.py:24
  316.4 6.0 copy-start.58
  399.2 8.9 %copy-start.5 = (f32[64,1,16,128]{3,0,2,1:T(8,128)S(1)}, f32[64,1,16,128]{3,0,2,1:T(8,128)}, u32[]{:S(2)}) copy-start(f32[64,1,16,128]{3,0,2,1:T(8,128)} %copy-done.4) | copy-start | bytes 1572868
  402.9 5.3 copy-start.21
  402.9 5.3 copy-start.26
  414.0 13.9 %copy-start.12 = (f32[64,1,16,128]{3,0,2,1:T(8,128)}, f32[64,1,16,128]{3,0,2,1:T(8,128)S(1)}, u32[]{:S(2)}) copy-start(f32[64,1,16,128]{3,0,2,1:T(8,128)S(1)} %fusion.109) | copy-start | bytes 1572868
  414.0 12.2 %collective-permute-start.7 = (f32[64,1,16,128]{3,0,2,1:T(8,128)S(1)}, f32[64,1,16,128]{3,0,2,1:T(8,128)S(1)}, u32[]{:S(2)}, u32[]{:S(2)}) collective-permute-start(f32[64,1,16,128]{3,0,2,1:T(8,128)S(1)} %fusion.109), channel_id=1, source_target_pairs={{4,0},{8,4},{12,8},{16,12},{20,16},{24,20},{28,24},{0,28},{5,1},{9... | collective-permute-start | bytes 1572872 | tf_op jit(solution)/shard_map/ppermute | solution.py:25
  415.7 12.2 %collective-permute-start.6 = (f32[64,1,16,128]{3,0,2,1:T(8,128)S(1)}, f32[64,1,16,128]{3,0,2,1:T(8,128)S(1)}, u32[]{:S(2)}, u32[]{:S(2)}) collective-permute-start(f32[64,1,16,128]{3,0,2,1:T(8,128)S(1)} %fusion.109), channel_id=1, source_target_pairs={{0,4},{4,8},{8,12},{12,16},{16,20},{20,24},{24,28},{28,0},{1,5},{5... | collective-permute-start | bytes 1572872 | tf_op jit(solution)/shard_map/ppermute | solution.py:24
  446.7 6.0 copy-start.62
  529.5 8.9 %copy-start.13 = (f32[64,1,16,128]{3,0,2,1:T(8,128)S(1)}, f32[64,1,16,128]{3,0,2,1:T(8,128)}, u32[]{:S(2)}) copy-start(f32[64,1,16,128]{3,0,2,1:T(8,128)} %copy-done.12) | copy-start | bytes 1572868
  533.1 5.3 copy-start.19
  533.1 5.3 copy-start.23
  (62 other events, 238.0 us)
where the time goes:
time: 643 us; the launch traced here: 634 us
  matrix products  197 us (31%)
  local copies, waits for them, and re-layouts  194 us (30%)
  other arithmetic  121 us (19%)
  blocking collectives  72.8 us (11%)
  waiting for transfers between devices  39.3 us (6%)
  starting transfers between devices  7.26 us (1%)
    dot_general x108, matrix products, apply_lattice(): jnp.dot(blocks[9 * offset + inner], source, precision=HIGH, preferred_ele...  192 us
    reshape x96, local copies, waits for them, and re-layouts, apply_lattice(): source = shifted[:, offset:offset + width_x].reshape(orbits, -1)  96.8 us
    reshape x30, other arithmetic, apply_lattice(): jnp.roll(grid_view, (-shift_y, -shift_z), axis=(3, 4))  72.6 us
    slice x32, local copies, waits for them, and re-layouts, apply_lattice(): source = shifted[:, offset:offset + width_x].reshape(orbits, -1)  52.7 us
    psum x1, blocking collectives, shards(): gram_matrix = lax.psum(inner_rows(by_cells, by_cells), ('cells', 'vecs'))  39.4 us
    concatenate x14, other arithmetic, apply_lattice(): jnp.roll(grid_view, (-shift_y, -shift_z), axis=(3, 4))  37.1 us
    ppermute x4, waiting for transfers between devices, with_halo(): after = lax.ppermute(initial, axis, down)  27.2 us
    slice x16, local copies, waits for them, and re-layouts, apply_lattice(): jnp.roll(grid_view, (-shift_y, -shift_z), axis=(3, 4))  18.1 us
  transfers between devices with their start and end apart: 8, of which 7 were waited for; matrix products, arithmetic and copies ran while one was open for 2% of the time, Pallas kernels for 0%

commit v1 on v0

--- a/solution.py
+++ b/solution.py
@@ -1,8 +1,11 @@
+import functools
 import math
 
 import jax
 import jax.numpy as jnp
 from jax import lax
+from jax.experimental import pallas as pl
+from jax.experimental.pallas import tpu as pltpu
 from jax.sharding import PartitionSpec as P
 
 NVEC = 64
@@ -83,10 +86,252 @@
     return lax.all_to_all(mixed, "vecs", split_axis=2, concat_axis=3, tiled=True)
 
 
+def split_pair(value):
+    high = value.astype(jnp.bfloat16)
+    low = (value - high.astype(jnp.float32)).astype(jnp.bfloat16)
+    return high, low
+
+
+def pack_kernel(dests, center_ref, vectors_ref, potential_ref, out_ref):
+    orbits = potential_ref.shape[0]
+    bundle = vectors_ref.shape[0] // orbits
+    own = bundle // dests
+    onsite = potential_ref[:, 0, :] - center_ref[0]
+    for n in range(bundle):
+        d, t = n // own, n % own
+        out_ref[d, t * orbits : (t + 1) * orbits, :] = vectors_ref[pl.ds(n, orbits, stride=bundle), :]
+    for d in range(dests):
+        out_ref[d, own * orbits :, :] = onsite
+
+
+def build_weights(hopping_ref, weights):
+    orbits = hopping_ref.shape[1]
+    for inner in range(9):
+        parts = []
+        for offset in range(3):
+            d = 9 * offset + inner
+            parts.append(0.5 * (hopping_ref[d] + hopping_ref[26 - d].T))
+        row = jnp.concatenate(parts, axis=1)
+        high = row.astype(jnp.bfloat16).astype(jnp.float32)
+        low = row - high
+        weights[inner * orbits : (inner + 1) * orbits, :] = jnp.concatenate(
+            [high, high, low], axis=1
+        ).astype(jnp.bfloat16)
+
+
+def gather_shifts(product, orbits):
+    lanes = product.shape[1]
+    z = lax.broadcasted_iota(jnp.int32, (orbits, lanes), 1) % NZ
+
+    def part(dy, dz):
+        if abs(dy) > 1:
+            return 0.0
+        at = (3 * (dy + 1) + dz + 1) * orbits
+        return product[at : at + orbits]
+
+    def moved(value, shift):
+        shift = shift % lanes
+        return pltpu.roll(value, shift, 1) if shift else value
+
+    total = part(0, 0) + moved(part(-1, 0), NZ) + moved(part(1, 0), -NZ)
+    for k in range(-2, 2):
+        chosen = jnp.where(z > 0, part(k, 1), part(k + 1, 1))
+        total = total + moved(chosen, -1 - NZ * k)
+    for k in range(-1, 3):
+        chosen = jnp.where(z < NZ - 1, part(k, -1), part(k - 1, -1))
+        total = total + moved(chosen, 1 - NZ * k)
+    return total
+
+
+def filter_kernel(own, peers, packed_ref, hopping_ref, out_ref, weights, fields, highs, lows):
+    planes = packed_ref.shape[0]
+    orbits = hopping_ref.shape[1]
+    lanes = packed_ref.shape[2]
+    rows = orbits // peers
+    build_weights(hopping_ref, weights)
+
+    def put(slot, x, value):
+        high, low = split_pair(value)
+        at = (x + 1) * orbits
+        if not isinstance(x, int):
+            at = pl.multiple_of(at, orbits)
+        highs[slot, pl.ds(at, orbits), :] = high
+        lows[slot, pl.ds(at, orbits), :] = low
+
+    def wrap(slot):
+        for ref in (highs, lows):
+            ref[slot, 0:orbits, :] = ref[slot, planes * orbits : (planes + 1) * orbits, :]
+            ref[slot, (planes + 1) * orbits :, :] = ref[slot, orbits : 2 * orbits, :]
+
+    for x in range(planes):
+        value = jnp.concatenate(
+            [packed_ref[x, t * orbits : (t + 1) * orbits, :] for t in range(own)], axis=1
+        )
+        fields[0, x] = value
+        put(0, x, value)
+    wrap(0)
+    for step in range(STEPS):
+        now, later = step % 2, (step + 1) % 2
+
+        def body(x, carry):
+            at = pl.ds(pl.multiple_of(x * orbits, orbits), 3 * orbits)
+            high, low = highs[now, at, :], lows[now, at, :]
+            source = jnp.concatenate([high, low, high], axis=0)
+            product = jnp.dot(weights[...], source, preferred_element_type=jnp.float32)
+            onsite = packed_ref[x, own * orbits :, :]
+            results = []
+            for t in range(own):
+                span = slice(t * lanes, (t + 1) * lanes)
+                applied = gather_shifts(product[:, span], orbits) + onsite * fields[now, x, :, span]
+                if step:
+                    applied = 2.0 * applied - fields[later, x, :, span]
+                results.append(applied)
+            if step < STEPS - 1:
+                value = jnp.concatenate(results, axis=1)
+                fields[later, x] = value
+                put(later, x, value)
+            else:
+                for t in range(own):
+                    for p in range(peers):
+                        out_ref[p * planes + x, t * rows : (t + 1) * rows, :] = results[t][
+                            p * rows : (p + 1) * rows
+                        ]
+            return carry
+
+        lax.fori_loop(0, planes, body, 0, unroll=2)
+        if step < STEPS - 1:
+            wrap(later)
+
+
+def exchange(axis, me, count, slots, send_sems, recv_sems):
+    def copy(hop):
+        peer = lax.rem(me + hop, count)
+        return pltpu.make_async_remote_copy(
+            src_ref=slots.at[me],
+            dst_ref=slots.at[me],
+            send_sem=send_sems.at[hop],
+            recv_sem=recv_sems.at[hop],
+            device_id={axis: peer},
+            device_id_type=pl.DeviceIdType.MESH,
+        )
+
+    copies = [copy(hop) for hop in range(1, count)]
+    for each in copies:
+        each.start()
+    for each in copies:
+        each.wait()
+    total = slots[0]
+    for i in range(1, count):
+        total = total + slots[i]
+    return total
+
+
+def mix_kernel(cells, peers, factor, field_ref, out_ref, first, second, s1, r1, s2, r2):
+    mine, place = lax.axis_index("vecs"), lax.axis_index("cells")
+    barrier = pltpu.get_barrier_semaphore()
+    for axis, me, count in (("vecs", mine, peers), ("cells", place, cells)):
+        for hop in range(1, count):
+            pl.semaphore_signal(
+                barrier,
+                inc=1,
+                device_id={axis: lax.rem(me + hop, count)},
+                device_id_type=pl.DeviceIdType.MESH,
+            )
+    rows, vectors = out_ref.shape[1], out_ref.shape[0] * out_ref.shape[2]
+    lanes, bundle, half = out_ref.shape[3], out_ref.shape[2], vectors // 2
+    field = jnp.concatenate(
+        [field_ref[pl.ds(o, vectors, stride=rows), :] for o in range(rows)], axis=1
+    )
+    gram = lax.dot_general(
+        field, field, (((1,), (1,)), ((), ())), precision=HIGH, preferred_element_type=jnp.float32
+    )
+    pl.semaphore_wait(barrier, peers + cells - 2)
+    first[mine] = jnp.concatenate([gram[:half], gram[half:]], axis=1)
+    second[place] = exchange("vecs", mine, peers, first, s1, r1)
+    total = exchange("cells", place, cells, second, s2, r2)
+    gram = jnp.concatenate([total[:, :vectors], total[:, vectors:]], axis=0)
+    frobenius = jnp.sqrt(jnp.sum(gram * gram, axis=(0, 1), keepdims=True))
+    row = lax.broadcasted_iota(jnp.int32, gram.shape, 0)
+    column = lax.broadcasted_iota(jnp.int32, gram.shape, 1)
+    unit = jnp.where(row == column, 1.5, 0.0)
+    mixing = (unit - 0.5 * gram / frobenius) / jnp.sqrt(frobenius)
+    mixed = lax.dot_general(
+        mixing, field, (((0,), (0,)), ((), ())), precision=HIGH, preferred_element_type=jnp.float32
+    )
+    for p in range(peers):
+        for o in range(rows):
+            out_ref[p, o] = (
+                mixed[p * bundle : (p + 1) * bundle, o * lanes : (o + 1) * lanes] * factor
+            )
+
+
+def resident_shards(vectors, potential, hopping, center):
+    orbits, _, bundle, lanes = vectors.shape
+    cells, peers = lax.axis_size("cells"), lax.axis_size("vecs")
+    own, rows, planes = bundle // cells, orbits // peers, cells
+    vmem, smem = pl.BlockSpec(memory_space=pltpu.VMEM), pl.BlockSpec(memory_space=pltpu.SMEM)
+    f32 = jnp.float32
+    packed = pl.pallas_call(
+        functools.partial(pack_kernel, cells),
+        out_shape=jax.ShapeDtypeStruct((cells, (own + 1) * orbits, lanes), f32),
+        in_specs=[smem, vmem, vmem],
+        out_specs=vmem,
+        name="pack",
+    )(center, vectors.reshape(orbits * bundle, lanes), potential)
+    packed = lax.all_to_all(packed, "cells", split_axis=0, concat_axis=0, tiled=True)
+    padded = (2, (planes + 2) * orbits, own * lanes)
+    filtered = pl.pallas_call(
+        functools.partial(filter_kernel, own, peers),
+        out_shape=jax.ShapeDtypeStruct((peers * planes, own * rows, lanes), f32),
+        in_specs=[vmem, vmem],
+        out_specs=vmem,
+        scratch_shapes=[
+            pltpu.VMEM((9 * orbits, 9 * orbits), jnp.bfloat16),
+            pltpu.VMEM((2, planes, orbits, own * lanes), f32),
+            pltpu.VMEM(padded, jnp.bfloat16),
+            pltpu.VMEM(padded, jnp.bfloat16),
+        ],
+        name="filter",
+    )(packed, hopping)
+    by_rows = lax.all_to_all(filtered, ("vecs", "cells"), split_axis=0, concat_axis=0, tiled=True)
+    count = bundle * peers
+    factor = math.sqrt(float(cells * lanes))
+    dma = pltpu.SemaphoreType.DMA
+    mixed = pl.pallas_call(
+        functools.partial(mix_kernel, cells, peers, factor),
+        out_shape=jax.ShapeDtypeStruct((peers, rows, bundle, lanes), f32),
+        in_specs=[vmem],
+        out_specs=vmem,
+        scratch_shapes=[
+            pltpu.VMEM((peers, count // 2, 2 * count), f32),
+            pltpu.VMEM((cells, count // 2, 2 * count), f32),
+            dma((peers,)),
+            dma((peers,)),
+            dma((cells,)),
+            dma((cells,)),
+        ],
+        compiler_params=pltpu.CompilerParams(collective_id=0, has_side_effects=True),
+        name="mix",
+    )(by_rows.reshape(count * rows, lanes))
+    result = lax.all_to_all(mixed, "vecs", split_axis=0, concat_axis=0, tiled=True)
+    return result.reshape(orbits, 1, bundle, lanes)
+
+
 def solution(mesh):
     placed = (P(None, "cells", "vecs", None), P(None, "cells", None), P(), P())
+
+    def body(vectors, potential, hopping, center):
+        _, width, bundle, merged = vectors.shape
+        fits = (
+            width == 1
+            and bundle % lax.axis_size("cells") == 0
+            and vectors.shape[0] % (8 * lax.axis_size("vecs")) == 0
+            and merged == 128
+        )
+        return (resident_shards if fits else shards)(vectors, potential, hopping, center)
+
     return jax.shard_map(
-        shards,
+        body,
         mesh=mesh,
         in_specs=placed,
         out_specs=P(None, "cells", "vecs", None),

time: 643 us -> 90.2 us (0.14); the launches traced: 634 us -> 89.8 us
  matrix products: 197 us -> 0 us
  local copies, waits for them, and re-layouts: 194 us -> 0.79 us
  other arithmetic: 121 us -> 0 us
  waiting for transfers between devices: 39.3 us -> 0 us
  Pallas kernels: 0 us -> 32 us
  blocking collectives: 72.8 us -> 56.4 us
  starting transfers between devices: 7.26 us -> 0 us
    dot_general x110 -> x0, matrix products: 197 us -> none  [the longest x108 192 us: apply_lattice(): jnp.dot(blocks[9 * offset + inner], source, precision=HIGH, preferred_ele...]
    reshape x96 -> x0, local copies, waits for them, and re-layouts: 96.8 us -> none  [apply_lattice(): source = shifted[:, offset:offset + width_x].reshape(orbits, -1)]
    reshape x31 -> x0, other arithmetic: 74 us -> none  [the longest x30 72.6 us: apply_lattice(): jnp.roll(grid_view, (-shift_y, -shift_z), axis=(3, 4))]
    slice x48 -> x0, local copies, waits for them, and re-layouts: 70.8 us -> none  [the longest x32 52.7 us: apply_lattice(): source = shifted[:, offset:offset + width_x].reshape(orbits, -1)]
    concatenate x17 -> x0, other arithmetic: 40.9 us -> none  [the longest x14 37.1 us: apply_lattice(): jnp.roll(grid_view, (-shift_y, -shift_z), axis=(3, 4))]
    psum x1 -> x0, blocking collectives: 39.4 us -> none  [shards(): gram_matrix = lax.psum(inner_rows(by_cells, by_cells), ('cells', 'vecs'))]
    ppermute x8 -> x0, waiting for transfers between devices: 39.3 us -> none  [the longest x4 27.2 us: with_halo(): after = lax.ppermute(initial, axis, down)]
    pallas_call x0 -> x3, Pallas kernels: none -> 32 us  [the longest x1 17.5 us: resident_shards(): pl.pallas_call(functools.partial(filter_kernel, own, peers), out_shape=ja...]
  transfers between devices with their start and end apart: 8 -> 0, of which waited for: 7 -> 0; matrix products, arithmetic and copies ran while one was open for 2% -> 0% of each run, Pallas kernels for 0% -> 0%
where the time goes in v1:
time: 90.2 us; the launch traced here: 89.8 us
  blocking collectives  56.4 us (63%)
  Pallas kernels  32 us (35%)
    all_to_all x1, blocking collectives, resident_shards(): lax.all_to_all(filtered, ('vecs', 'cells'), split_axis=0, concat_axis=0,...  20.1 us
    all_to_all x1, blocking collectives, resident_shards(): lax.all_to_all(mixed, 'vecs', split_axis=0, concat_axis=0, tiled=True)  18.5 us
    all_to_all x1, blocking collectives, resident_shards(): lax.all_to_all(packed, 'cells', split_axis=0, concat_axis=0, tiled=True)  17.8 us
    pallas_call x1, Pallas kernels, resident_shards(): pl.pallas_call(functools.partial(filter_kernel, own, peers), out_shape=ja...  17.5 us
    pallas_call x1, Pallas kernels, resident_shards(): pl.pallas_call(functools.partial(mix_kernel, cells, peers, factor), out_s...  12.4 us
    pallas_call x1, Pallas kernels, resident_shards(): pl.pallas_call(functools.partial(pack_kernel, cells), out_shape=jax.Shape...  2.11 us

profile of v1, /device:TPU:0, one launch (start us, length us, event | category | flops | bytes accessed | tf_op | source)
XLA Modules:
  0.0 89.8 jit_solution(8242430164441194785)
XLA Ops:
  0.7 2.1 %pack.1 = f32[8,192,128]{2,1,0:T(8,128)} custom-call(f32[1]{0:T(128)S(6)} %copy.7.center_ref, f32[1024,128]{1,0:T(8,128)} %bitcast.7, f32[64,1,128]{2,1,0:T(1,128)} %potential_ref.1), custom_call_target="tpu_custom_call" | custom-call | tf_op jit(solution)/shard_map/pack/pallas_call | solution.py:274
  2.8 17.8 %all_to_all.15.packed_ref = f32[8,192,128]{2,1,0:T(8,128)} all-to-all(f32[8,192,128]{2,1,0:T(8,128)} %pack.1), channel_id=1, replica_groups=mesh['cells'=8,'vecs'=4] {'cells'}, dimensions={0} | all-to-all | bytes 1572864 | tf_op jit(solution)/shard_map/all_to_all | solution.py:281
  20.6 17.5 %filter.1 = f32[32,32,128]{2,1,0:T(8,128)} custom-call(f32[8,192,128]{2,1,0:T(8,128)} %all_to_all.15.packed_ref, f32[27,64,64]{2,1,0:T(8,128)} %hopping_ref.1), custom_call_target="tpu_custom_call" | custom-call | tf_op jit(solution)/shard_map/filter/pallas_call | solution.py:283
  38.1 20.1 %all_to_all.16 = f32[32,32,128]{2,1,0:T(8,128)} all-to-all(f32[32,32,128]{2,1,0:T(8,128)} %filter.1), channel_id=1, replica_groups=mesh['cells'=8,'vecs'=4] {'vecs','cells'}, dimensions={0} | all-to-all | bytes 1048576 | tf_op jit(solution)/shard_map/all_to_all | solution.py:296
  58.2 12.4 %mix.1 = f32[4,16,16,128]{3,2,1,0:T(8,128)} custom-call(f32[1024,128]{1,0:T(8,128)} %bitcast.5), custom_call_target="tpu_custom_call" | custom-call | tf_op jit(solution)/shard_map/mix/pallas_call | solution.py:300
  70.5 18.5 %all_to_all.17 = f32[4,16,16,128]{3,2,1,0:T(8,128)S(1)} all-to-all(f32[4,16,16,128]{3,2,1,0:T(8,128)} %mix.1), channel_id=1, replica_groups=mesh['cells'=8,'vecs'=4] {'vecs'}, dimensions={0} | all-to-all | bytes 1048576 | tf_op jit(solution)/shard_map/all_to_all | solution.py:316
  89.0 0.8 copy.8

commit v2 on v0

--- a/solution.py
+++ b/solution.py
@@ -1,8 +1,11 @@
+import functools
 import math
 
 import jax
 import jax.numpy as jnp
 from jax import lax
+from jax.experimental import pallas as pl
+from jax.experimental.pallas import tpu as pltpu
 from jax.sharding import PartitionSpec as P
 
 NVEC = 64
@@ -83,10 +86,291 @@
     return lax.all_to_all(mixed, "vecs", split_axis=2, concat_axis=3, tiled=True)
 
 
+def split_pair(value):
+    high = value.astype(jnp.bfloat16)
+    low = (value - high.astype(jnp.float32)).astype(jnp.bfloat16)
+    return high, low
+
+
+def build_weights(hopping_ref, weights):
+    orbits = hopping_ref.shape[1]
+    for inner in range(9):
+        parts = []
+        for offset in range(3):
+            d = 9 * offset + inner
+            parts.append(0.5 * (hopping_ref[d] + hopping_ref[26 - d].T))
+        row = jnp.concatenate(parts, axis=1)
+        high = row.astype(jnp.bfloat16).astype(jnp.float32)
+        low = row - high
+        weights[inner * orbits : (inner + 1) * orbits, :] = jnp.concatenate(
+            [high, high, low], axis=1
+        ).astype(jnp.bfloat16)
+
+
+def gather_shifts(product, orbits):
+    lanes = product.shape[1]
+    z = lax.broadcasted_iota(jnp.int32, (orbits, lanes), 1) % NZ
+
+    def part(dy, dz):
+        if abs(dy) > 1:
+            return 0.0
+        at = (3 * (dy + 1) + dz + 1) * orbits
+        return product[at : at + orbits]
+
+    def moved(value, shift):
+        shift = shift % lanes
+        return pltpu.roll(value, shift, 1) if shift else value
+
+    total = part(0, 0) + moved(part(-1, 0), NZ) + moved(part(1, 0), -NZ)
+    for k in range(-2, 2):
+        chosen = jnp.where(z > 0, part(k, 1), part(k + 1, 1))
+        total = total + moved(chosen, -1 - NZ * k)
+    for k in range(-1, 3):
+        chosen = jnp.where(z < NZ - 1, part(k, -1), part(k - 1, -1))
+        total = total + moved(chosen, 1 - NZ * k)
+    return total
+
+
+def remote(source, target, send, receive, device):
+    return pltpu.make_async_remote_copy(
+        src_ref=source,
+        dst_ref=target,
+        send_sem=send,
+        recv_sem=receive,
+        device_id=device,
+        device_id_type=pl.DeviceIdType.MESH,
+    )
+
+
+def exchange(axis, me, count, slots, send_sems, recv_sems):
+    copies = [
+        remote(
+            slots.at[me],
+            slots.at[me],
+            send_sems.at[hop],
+            recv_sems.at[hop],
+            {axis: lax.rem(me + hop, count)},
+        )
+        for hop in range(1, count)
+    ]
+    for each in copies:
+        each.start()
+    for each in copies:
+        each.wait()
+    total = slots[0]
+    for i in range(1, count):
+        total = total + slots[i]
+    return total
+
+
+def whole_kernel(
+    cells, peers, factor,
+    center_ref, vectors_ref, potential_ref, hopping_ref, out_ref,
+    packed, arrived, weights, fields, highs, lows, leaving, by_rows, first, second, mixed,
+    s1, r1, s2, r2, s3, r3, s4, r4, s5, r5,
+):
+    mine, place = lax.axis_index("vecs"), lax.axis_index("cells")
+    orbits, lanes = hopping_ref.shape[1], packed.shape[2]
+    bundle = vectors_ref.shape[0] // orbits
+    own, rows, planes = bundle // cells, orbits // peers, cells
+    vectors = bundle * peers
+    me = mine * cells + place
+
+    barrier = pltpu.get_barrier_semaphore()
+    for hop in range(cells):
+        for turn in range(peers):
+            if hop or turn:
+                pl.semaphore_signal(
+                    barrier,
+                    inc=1,
+                    device_id={
+                        "cells": lax.rem(place + hop, cells),
+                        "vecs": lax.rem(mine + turn, peers),
+                    },
+                    device_id_type=pl.DeviceIdType.MESH,
+                )
+
+    onsite = potential_ref[:, 0, :] - center_ref[0]
+    for n in range(bundle):
+        d, t = n // own, n % own
+        packed[d, t * orbits : (t + 1) * orbits, :] = vectors_ref[pl.ds(n, orbits, stride=bundle), :]
+    for d in range(cells):
+        packed[d, own * orbits :, :] = onsite
+    pl.semaphore_wait(barrier, cells * peers - 1)
+    copies = []
+    for hop in range(1, cells):
+        peer = lax.rem(place + hop, cells)
+        copies.append(
+            remote(packed.at[peer], arrived.at[place], s1.at[hop], r1.at[hop], {"cells": peer})
+        )
+    for each in copies:
+        each.start()
+    arrived[place] = packed[place]
+    build_weights(hopping_ref, weights)
+    for each in copies:
+        each.wait()
+
+    def put(slot, x, value):
+        high, low = split_pair(value)
+        at = (x + 1) * orbits
+        if not isinstance(x, int):
+            at = pl.multiple_of(at, orbits)
+        highs[slot, pl.ds(at, orbits), :] = high
+        lows[slot, pl.ds(at, orbits), :] = low
+
+    def wrap(slot):
+        for ref in (highs, lows):
+            ref[slot, 0:orbits, :] = ref[slot, planes * orbits : (planes + 1) * orbits, :]
+            ref[slot, (planes + 1) * orbits :, :] = ref[slot, orbits : 2 * orbits, :]
+
+    for x in range(planes):
+        value = jnp.concatenate(
+            [arrived[x, t * orbits : (t + 1) * orbits, :] for t in range(own)], axis=1
+        )
+        fields[0, x] = value
+        put(0, x, value)
+    wrap(0)
+
+    def advance(step, x):
+        now, later = step % 2, (step + 1) % 2
+        at = pl.ds(pl.multiple_of(x * orbits, orbits), 3 * orbits)
+        high, low = highs[now, at, :], lows[now, at, :]
+        source = jnp.concatenate([high, low, high], axis=0)
+        product = jnp.dot(weights[...], source, preferred_element_type=jnp.float32)
+        onsite = arrived[x, own * orbits :, :]
+        results = []
+        for t in range(own):
+            span = slice(t * lanes, (t + 1) * lanes)
+            applied = gather_shifts(product[:, span], orbits) + onsite * fields[now, x, :, span]
+            if step:
+                applied = 2.0 * applied - fields[later, x, :, span]
+            results.append(applied)
+        return results
+
+    for step in range(STEPS - 1):
+        later = (step + 1) % 2
+
+        def body(x, carry):
+            value = jnp.concatenate(advance(step, x), axis=1)
+            fields[later, x] = value
+            put(later, x, value)
+            return carry
+
+        lax.fori_loop(0, planes, body, 0, unroll=2)
+        wrap(later)
+
+    copies = []
+    for hop in list(range(1, planes)) + [0]:
+        x = lax.rem(place + hop, planes)
+        results = advance(STEPS - 1, x)
+        for t in range(own):
+            for p in range(peers):
+                leaving[hop, p, t * rows : (t + 1) * rows, :] = results[t][p * rows : (p + 1) * rows]
+        for turn in range(1, peers) if hop == 0 else range(peers):
+            p = lax.rem(mine + turn, peers)
+            sem = hop * peers + turn
+            copy = remote(
+                leaving.at[hop, p], by_rows.at[me], s2.at[sem], r2.at[sem], {"cells": x, "vecs": p}
+            )
+            copy.start()
+            copies.append(copy)
+    by_rows[me] = leaving[0, mine]
+    for each in copies:
+        each.wait()
+
+    flat = by_rows.reshape(vectors * rows, lanes)
+    field = jnp.concatenate(
+        [flat[pl.ds(o, vectors, stride=rows), :] for o in range(rows)], axis=1
+    )
+    high, low = split_pair(field)
+    both = lax.dot_general(
+        jnp.concatenate([high, low], axis=0),
+        high,
+        (((1,), (1,)), ((), ())),
+        preferred_element_type=jnp.float32,
+    )
+    cross = both[vectors:]
+    gram = both[:vectors] + cross + cross.T
+    half = vectors // 2
+    first[mine] = jnp.concatenate([gram[:half], gram[half:]], axis=1)
+    second[place] = exchange("vecs", mine, peers, first, s3, r3)
+    total = exchange("cells", place, cells, second, s4, r4)
+    gram = jnp.concatenate([total[:, :vectors], total[:, vectors:]], axis=0)
+    frobenius = jnp.sqrt(jnp.sum(gram * gram, axis=(0, 1), keepdims=True))
+    row = lax.broadcasted_iota(jnp.int32, gram.shape, 0)
+    column = lax.broadcasted_iota(jnp.int32, gram.shape, 1)
+    unit = jnp.where(row == column, 1.5, 0.0)
+    mixing = (unit - 0.5 * gram / frobenius) / jnp.sqrt(frobenius)
+    mixing_high, mixing_low = split_pair(mixing.T)
+    result = factor * jnp.dot(
+        jnp.concatenate([mixing_high, mixing_high, mixing_low], axis=1),
+        jnp.concatenate([high, low, high], axis=0),
+        preferred_element_type=jnp.float32,
+    )
+    for p in range(peers):
+        for o in range(rows):
+            mixed[p, o] = result[p * bundle : (p + 1) * bundle, o * lanes : (o + 1) * lanes]
+    copies = []
+    for turn in range(1, peers):
+        p = lax.rem(mine + turn, peers)
+        copies.append(remote(mixed.at[p], out_ref.at[mine], s5.at[turn], r5.at[turn], {"vecs": p}))
+    for each in copies:
+        each.start()
+    out_ref[mine] = mixed[mine]
+    for each in copies:
+        each.wait()
+
+
+def resident_shards(vectors, potential, hopping, center):
+    orbits, _, bundle, lanes = vectors.shape
+    cells, peers = lax.axis_size("cells"), lax.axis_size("vecs")
+    own, rows, planes = bundle // cells, orbits // peers, cells
+    count = bundle * peers
+    vmem, smem = pl.BlockSpec(memory_space=pltpu.VMEM), pl.BlockSpec(memory_space=pltpu.SMEM)
+    f32, bf16, dma = jnp.float32, jnp.bfloat16, pltpu.SemaphoreType.DMA
+    sizes = [n for n in (cells, cells * peers, peers, cells, peers) for _ in range(2)]
+    result = pl.pallas_call(
+        functools.partial(whole_kernel, cells, peers, math.sqrt(float(cells * lanes))),
+        out_shape=jax.ShapeDtypeStruct((peers, rows, bundle, lanes), f32),
+        in_specs=[smem, vmem, vmem, vmem],
+        out_specs=vmem,
+        scratch_shapes=[
+            pltpu.VMEM((cells, (own + 1) * orbits, lanes), f32),
+            pltpu.VMEM((cells, (own + 1) * orbits, lanes), f32),
+            pltpu.VMEM((9 * orbits, 9 * orbits), bf16),
+            pltpu.VMEM((2, planes, orbits, own * lanes), f32),
+            pltpu.VMEM((2, (planes + 2) * orbits, own * lanes), bf16),
+            pltpu.VMEM((2, (planes + 2) * orbits, own * lanes), bf16),
+            pltpu.VMEM((planes, peers, own * rows, lanes), f32),
+            pltpu.VMEM((peers * planes, own * rows, lanes), f32),
+            pltpu.VMEM((peers, count // 2, 2 * count), f32),
+            pltpu.VMEM((cells, count // 2, 2 * count), f32),
+            pltpu.VMEM((peers, rows, bundle, lanes), f32),
+        ]
+        + [dma((n,)) for n in sizes],
+        compiler_params=pltpu.CompilerParams(
+            collective_id=0, has_side_effects=True, vmem_limit_bytes=48 * 1024 * 1024
+        ),
+        name="whole",
+    )(center, vectors.reshape(orbits * bundle, lanes), potential, hopping)
+    return result.reshape(orbits, 1, bundle, lanes)
+
+
 def solution(mesh):
     placed = (P(None, "cells", "vecs", None), P(None, "cells", None), P(), P())
+
+    def body(vectors, potential, hopping, center):
+        _, width, bundle, merged = vectors.shape
+        fits = (
+            width == 1
+            and bundle % lax.axis_size("cells") == 0
+            and vectors.shape[0] % (8 * lax.axis_size("vecs")) == 0
+            and merged == 128
+        )
+        return (resident_shards if fits else shards)(vectors, potential, hopping, center)
+
     return jax.shard_map(
-        shards,
+        body,
         mesh=mesh,
         in_specs=placed,
         out_specs=P(None, "cells", "vecs", None),

time: 643 us -> 66.1 us (0.10); the launches traced: 634 us -> 65.8 us
  matrix products: 197 us -> 0 us
  local copies, waits for them, and re-layouts: 194 us -> 3.75 us
  other arithmetic: 121 us -> 0 us
  blocking collectives: 72.8 us -> 0 us
  Pallas kernels: 0 us -> 61.4 us
  waiting for transfers between devices: 39.3 us -> 0 us
  starting transfers between devices: 7.26 us -> 0 us
    dot_general x110 -> x0, matrix products: 197 us -> none  [the longest x108 192 us: apply_lattice(): jnp.dot(blocks[9 * offset + inner], source, precision=HIGH, preferred_ele...]
    reshape x96 -> x0, local copies, waits for them, and re-layouts: 96.8 us -> none  [apply_lattice(): source = shifted[:, offset:offset + width_x].reshape(orbits, -1)]
    reshape x31 -> x0, other arithmetic: 74 us -> none  [the longest x30 72.6 us: apply_lattice(): jnp.roll(grid_view, (-shift_y, -shift_z), axis=(3, 4))]
    slice x48 -> x0, local copies, waits for them, and re-layouts: 70.8 us -> none  [the longest x32 52.7 us: apply_lattice(): source = shifted[:, offset:offset + width_x].reshape(orbits, -1)]
    pallas_call x0 -> x1, Pallas kernels: none -> 61.4 us  [resident_shards(): pl.pallas_call(functools.partial(whole_kernel, cells, peers, math.sqrt(fl...]
    concatenate x17 -> x0, other arithmetic: 40.9 us -> none  [the longest x14 37.1 us: apply_lattice(): jnp.roll(grid_view, (-shift_y, -shift_z), axis=(3, 4))]
    psum x1 -> x0, blocking collectives: 39.4 us -> none  [shards(): gram_matrix = lax.psum(inner_rows(by_cells, by_cells), ('cells', 'vecs'))]
    ppermute x8 -> x0, waiting for transfers between devices: 39.3 us -> none  [the longest x4 27.2 us: with_halo(): after = lax.ppermute(initial, axis, down)]
  transfers between devices with their start and end apart: 8 -> 0, of which waited for: 7 -> 0; matrix products, arithmetic and copies ran while one was open for 2% -> 0% of each run, Pallas kernels for 0% -> 0%
where the time goes in v2:
time: 66.1 us; the launch traced here: 65.8 us
  Pallas kernels  61.4 us (93%)
  local copies, waits for them, and re-layouts  3.75 us (6%)
  between operations  0.67 us (1%)
    pallas_call x1, Pallas kernels, resident_shards(): pl.pallas_call(functools.partial(whole_kernel, cells, peers, math.sqrt(fl...  61.4 us
    unnamed x7, local copies, waits for them, and re-layouts  3.75 us

profile of v2, /device:TPU:0, one launch (start us, length us, event | category | flops | bytes accessed | tf_op | source)
XLA Modules:
  0.0 65.8 jit_solution(15802381430268529686)
XLA Ops:
  0.7 0.0 copy-start
  0.7 1.2 %copy-done = f32[27,64,64]{2,1,0:T(8,128)S(1)} copy-done((f32[27,64,64]{2,1,0:T(8,128)S(1)}, f32[27,64,64]{2,1,0:T(8,128)}, u32[]{:S(2)}) %copy-start) | copy-done | bytes 442392
  1.8 0.0 copy-start.1
  1.8 1.0 %copy-done.1 = f32[64,1,16,128]{3,2,1,0:T(8,128)S(1)} copy-done((f32[64,1,16,128]{3,2,1,0:T(8,128)S(1)}, f32[64,1,16,128]{3,2,1,0:T(8,128)}, u32[]{:S(2)}) %copy-start.1) | copy-done | bytes 524312
  2.9 0.0 copy-start.2
  2.9 0.8 %copy-done.2 = f32[64,1,128]{2,1,0:T(1,128)S(1)} copy-done((f32[64,1,128]{2,1,0:T(1,128)S(1)}, f32[64,1,128]{2,1,0:T(1,128)}, u32[]{:S(2)}) %copy-start.2) | copy-done | bytes 32792
  3.6 61.4 %whole.1 = f32[4,16,16,128]{3,2,1,0:T(8,128)S(1)} custom-call(f32[1]{0:T(128)S(6)} %copy.7.center_ref, f32[1024,128]{1,0:T(8,128)S(1)} %bitcast.5, f32[64,1,128]{2,1,0:T(1,128)S(1)} %copy-done.2, f32[27,64,64]{2,1,0:T(8,128)S(1)} %copy-done), custom_call_target="tpu_custom_call" | custom-call | tf_op jit(solution)/shard_map/whole/pallas_call | solution.py:332
  65.0 0.8 %copy.8 = f32[64,1,16,128]{3,2,1,0:T(8,128)} copy(f32[64,1,16,128]{3,2,1,0:T(8,128)S(1)} %bitcast.4) | data formatting | bytes 1048576
Async XLA Ops:
  0.7 1.2 %copy-start = (f32[27,64,64]{2,1,0:T(8,128)S(1)}, f32[27,64,64]{2,1,0:T(8,128)}, u32[]{:S(2)}) copy-start(f32[27,64,64]{2,1,0:T(8,128)} %hopping_ref.1) | copy-start | bytes 1327108
  1.8 1.0 %copy-start.1 = (f32[64,1,16,128]{3,2,1,0:T(8,128)S(1)}, f32[64,1,16,128]{3,2,1,0:T(8,128)}, u32[]{:S(2)}) copy-start(f32[64,1,16,128]{3,2,1,0:T(8,128)} %param.4) | copy-start | bytes 1572868
  2.9 0.8 %copy-start.2 = (f32[64,1,128]{2,1,0:T(1,128)S(1)}, f32[64,1,128]{2,1,0:T(1,128)}, u32[]{:S(2)}) copy-start(f32[64,1,128]{2,1,0:T(1,128)} %potential_ref.1) | copy-start | bytes 98308

commit v3 on v2

--- a/solution.py
+++ b/solution.py
@@ -163,11 +163,29 @@
     return total
 
 
+def demand_order(planes):
+    order, known = [], {(0, x) for x in range(planes)}
+
+    def need(step, x):
+        if (step, x) in known:
+            return
+        for near in (-1, 0, 1):
+            need(step - 1, (x + near) % planes)
+        known.add((step, x))
+        order.append((step, x))
+
+    for x in list(range(1, planes)) + [0]:
+        need(STEPS, x)
+    return order
+
+
 def whole_kernel(
     cells, peers, factor,
-    center_ref, vectors_ref, potential_ref, hopping_ref, out_ref,
-    packed, arrived, weights, fields, highs, lows, leaving, by_rows, first, second, mixed,
-    s1, r1, s2, r2, s3, r3, s4, r4, s5, r5,
+    center_ref, vectors_any, potential_any, hopping_any, out_ref,
+    vectors_ref, potential_ref, hopping_ref,
+    packed, onsite_ref, planes_in, onsite_in, weights, fields, highs, lows, leaving, by_rows,
+    first, second, mixed,
+    local, s1, r1, s6, r6, s2, r2, s3, r3, s4, r4, s5, r5,
 ):
     mine, place = lax.axis_index("vecs"), lax.axis_index("cells")
     orbits, lanes = hopping_ref.shape[1], packed.shape[2]
@@ -176,6 +194,18 @@
     vectors = bundle * peers
     me = mine * cells + place
 
+    loads = [
+        pltpu.make_async_copy(source, target, local.at[n])
+        for n, (source, target) in enumerate(
+            (
+                (vectors_any, vectors_ref),
+                (potential_any, potential_ref),
+                (hopping_any, hopping_ref),
+            )
+        )
+    ]
+    for each in loads:
+        each.start()
     barrier = pltpu.get_barrier_semaphore()
     for hop in range(cells):
         for turn in range(peers):
@@ -190,91 +220,101 @@
                     device_id_type=pl.DeviceIdType.MESH,
                 )
 
-    onsite = potential_ref[:, 0, :] - center_ref[0]
+    loads[0].wait()
     for n in range(bundle):
         d, t = n // own, n % own
         packed[d, t * orbits : (t + 1) * orbits, :] = vectors_ref[pl.ds(n, orbits, stride=bundle), :]
-    for d in range(cells):
-        packed[d, own * orbits :, :] = onsite
+    loads[1].wait()
+    onsite = potential_ref[:, 0, :] - center_ref[0]
+    onsite_ref[...] = onsite
+    onsite_in[0] = onsite
+
+    order = demand_order(planes)
+    sequence = []
+    for step, x in order:
+        if step == 1:
+            wanted = [("plane", (x + near) % planes) for near in (-1, 0, 1)] + [("onsite", x)]
+            sequence += [item for item in wanted if item[1] and item not in sequence]
+    arriving = {}
     pl.semaphore_wait(barrier, cells * peers - 1)
-    copies = []
-    for hop in range(1, cells):
+    for kind, slot in sequence:
+        hop = planes - slot
         peer = lax.rem(place + hop, cells)
-        copies.append(
-            remote(packed.at[peer], arrived.at[place], s1.at[hop], r1.at[hop], {"cells": peer})
-        )
-    for each in copies:
-        each.start()
-    arrived[place] = packed[place]
+        if kind == "plane":
+            copy = remote(
+                packed.at[peer], planes_in.at[slot], s1.at[hop], r1.at[hop], {"cells": peer}
+            )
+        else:
+            copy = remote(onsite_ref, onsite_in.at[slot], s6.at[hop], r6.at[hop], {"cells": peer})
+        copy.start()
+        arriving[kind, slot] = copy
+    sent = list(arriving.values())
+    loads[2].wait()
     build_weights(hopping_ref, weights)
-    for each in copies:
-        each.wait()
 
     def put(slot, x, value):
+        fields[slot, x] = value
         high, low = split_pair(value)
-        at = (x + 1) * orbits
-        if not isinstance(x, int):
-            at = pl.multiple_of(at, orbits)
-        highs[slot, pl.ds(at, orbits), :] = high
-        lows[slot, pl.ds(at, orbits), :] = low
-
-    def wrap(slot):
-        for ref in (highs, lows):
-            ref[slot, 0:orbits, :] = ref[slot, planes * orbits : (planes + 1) * orbits, :]
-            ref[slot, (planes + 1) * orbits :, :] = ref[slot, orbits : 2 * orbits, :]
-
-    for x in range(planes):
-        value = jnp.concatenate(
-            [arrived[x, t * orbits : (t + 1) * orbits, :] for t in range(own)], axis=1
-        )
-        fields[0, x] = value
-        put(0, x, value)
-    wrap(0)
+        highs[slot, x], lows[slot, x] = high, low
+
+    ready = set()
+
+    def receive(x):
+        if x in ready:
+            return
+        ready.add(x)
+        if x:
+            arriving["plane", x].wait_recv()
+            pieces = [planes_in[x, t * orbits : (t + 1) * orbits, :] for t in range(own)]
+        else:
+            pieces = [packed[place, t * orbits : (t + 1) * orbits, :] for t in range(own)]
+        put(0, x, jnp.concatenate(pieces, axis=1))
 
     def advance(step, x):
-        now, later = step % 2, (step + 1) % 2
-        at = pl.ds(pl.multiple_of(x * orbits, orbits), 3 * orbits)
-        high, low = highs[now, at, :], lows[now, at, :]
-        source = jnp.concatenate([high, low, high], axis=0)
+        now, later = (step - 1) % 2, step % 2
+        around = [(x + near) % planes for near in (-1, 0, 1)]
+        high, low = [highs[now, r] for r in around], [lows[now, r] for r in around]
+        source = jnp.concatenate(high + low + high, axis=0)
         product = jnp.dot(weights[...], source, preferred_element_type=jnp.float32)
-        onsite = arrived[x, own * orbits :, :]
+        onsite = onsite_in[x]
         results = []
         for t in range(own):
             span = slice(t * lanes, (t + 1) * lanes)
             applied = gather_shifts(product[:, span], orbits) + onsite * fields[now, x, :, span]
-            if step:
+            if step > 1:
                 applied = 2.0 * applied - fields[later, x, :, span]
             results.append(applied)
         return results
 
-    for step in range(STEPS - 1):
-        later = (step + 1) % 2
-
-        def body(x, carry):
-            value = jnp.concatenate(advance(step, x), axis=1)
-            fields[later, x] = value
-            put(later, x, value)
-            return carry
-
-        lax.fori_loop(0, planes, body, 0, unroll=2)
-        wrap(later)
-
     copies = []
-    for hop in list(range(1, planes)) + [0]:
-        x = lax.rem(place + hop, planes)
-        results = advance(STEPS - 1, x)
+    for step, x in order:
+        if step == 1:
+            for near in (-1, 0, 1):
+                receive((x + near) % planes)
+            if x:
+                arriving["onsite", x].wait_recv()
+        results = advance(step, x)
+        if step < STEPS:
+            put(step % 2, x, jnp.concatenate(results, axis=1))
+            continue
         for t in range(own):
             for p in range(peers):
-                leaving[hop, p, t * rows : (t + 1) * rows, :] = results[t][p * rows : (p + 1) * rows]
-        for turn in range(1, peers) if hop == 0 else range(peers):
+                leaving[x, p, t * rows : (t + 1) * rows, :] = results[t][p * rows : (p + 1) * rows]
+        for turn in range(1, peers) if x == 0 else range(peers):
             p = lax.rem(mine + turn, peers)
-            sem = hop * peers + turn
+            sem = x * peers + turn
             copy = remote(
-                leaving.at[hop, p], by_rows.at[me], s2.at[sem], r2.at[sem], {"cells": x, "vecs": p}
+                leaving.at[x, p],
+                by_rows.at[me],
+                s2.at[sem],
+                r2.at[sem],
+                {"cells": lax.rem(place + x, cells), "vecs": p},
             )
             copy.start()
             copies.append(copy)
     by_rows[me] = leaving[0, mine]
+    for each in sent:
+        each.wait_send()
     for each in copies:
         each.wait()
 
@@ -327,29 +367,36 @@
     own, rows, planes = bundle // cells, orbits // peers, cells
     count = bundle * peers
     vmem, smem = pl.BlockSpec(memory_space=pltpu.VMEM), pl.BlockSpec(memory_space=pltpu.SMEM)
+    held = pl.BlockSpec(memory_space=pl.ANY)
     f32, bf16, dma = jnp.float32, jnp.bfloat16, pltpu.SemaphoreType.DMA
-    sizes = [n for n in (cells, cells * peers, peers, cells, peers) for _ in range(2)]
+    sizes = [n for n in (cells, cells, cells * peers, peers, cells, peers) for _ in range(2)]
     result = pl.pallas_call(
         functools.partial(whole_kernel, cells, peers, math.sqrt(float(cells * lanes))),
         out_shape=jax.ShapeDtypeStruct((peers, rows, bundle, lanes), f32),
-        in_specs=[smem, vmem, vmem, vmem],
+        in_specs=[smem, held, held, held],
         out_specs=vmem,
         scratch_shapes=[
-            pltpu.VMEM((cells, (own + 1) * orbits, lanes), f32),
-            pltpu.VMEM((cells, (own + 1) * orbits, lanes), f32),
+            pltpu.VMEM((orbits * bundle, lanes), f32),
+            pltpu.VMEM(potential.shape, f32),
+            pltpu.VMEM(hopping.shape, f32),
+            pltpu.VMEM((cells, own * orbits, lanes), f32),
+            pltpu.VMEM((orbits, lanes), f32),
+            pltpu.VMEM((cells, own * orbits, lanes), f32),
+            pltpu.VMEM((cells, orbits, lanes), f32),
             pltpu.VMEM((9 * orbits, 9 * orbits), bf16),
             pltpu.VMEM((2, planes, orbits, own * lanes), f32),
-            pltpu.VMEM((2, (planes + 2) * orbits, own * lanes), bf16),
-            pltpu.VMEM((2, (planes + 2) * orbits, own * lanes), bf16),
+            pltpu.VMEM((2, planes, orbits, own * lanes), bf16),
+            pltpu.VMEM((2, planes, orbits, own * lanes), bf16),
             pltpu.VMEM((planes, peers, own * rows, lanes), f32),
             pltpu.VMEM((peers * planes, own * rows, lanes), f32),
             pltpu.VMEM((peers, count // 2, 2 * count), f32),
             pltpu.VMEM((cells, count // 2, 2 * count), f32),
             pltpu.VMEM((peers, rows, bundle, lanes), f32),
         ]
+        + [dma((3,))]
         + [dma((n,)) for n in sizes],
         compiler_params=pltpu.CompilerParams(
-            collective_id=0, has_side_effects=True, vmem_limit_bytes=48 * 1024 * 1024
+            collective_id=0, has_side_effects=True, vmem_limit_bytes=62 * 1024 * 1024
         ),
         name="whole",
     )(center, vectors.reshape(orbits * bundle, lanes), potential, hopping)

time: 66.1 us -> 65.6 us (level)
  local copies, waits for them, and re-layouts: 3.75 us -> 1.87 us
  Pallas kernels: 61.4 us -> 62.4 us
    unnamed x7 -> x1, local copies, waits for them, and re-layouts: 3.75 us -> 1.87 us
    pallas_call x1, Pallas kernels: 61.4 us -> 62.4 us  [resident_shards(): pl.pallas_call(functools.partial(whole_kernel, cells, peers, math.sqrt(fl...]
where the time goes in v3:
time: 65.6 us; the launch traced here: 64.9 us
  Pallas kernels  62.4 us (95%)
  local copies, waits for them, and re-layouts  1.87 us (3%)
  between operations  0.66 us (1%)
    pallas_call x1, Pallas kernels, resident_shards(): pl.pallas_call(functools.partial(whole_kernel, cells, peers, math.sqrt(fl...  62.4 us
    unnamed x1, local copies, waits for them, and re-layouts  1.87 us

profile of v3, /device:TPU:0, one launch (start us, length us, event | category | flops | bytes accessed | tf_op | source)
XLA Modules:
  0.0 64.9 jit_solution(7617444934567756593)
XLA Ops:
  0.7 62.4 %whole.1 = f32[4,16,16,128]{3,2,1,0:T(8,128)} custom-call(f32[1]{0:T(128)S(6)} %copy.7.center_ref, f32[1024,128]{1,0:T(8,128)} %bitcast.5, f32[64,1,128]{2,1,0:T(1,128)} %potential_any.1, f32[27,64,64]{2,1,0:T(8,128)} %hopping_any.1), custom_call_target="tpu_custom_call" | custom-call | tf_op jit(solution)/shard_map/whole/pallas_call | solution.py:373
  63.0 1.9 %copy.8 = f32[64,1,16,128]{3,2,1,0:T(8,128)} copy(f32[64,1,16,128]{3,2,1,0:T(8,128)} %bitcast.4) | data formatting | bytes 1048576

commit v4 on v3

--- a/solution.py
+++ b/solution.py
@@ -164,7 +164,7 @@
 
 
 def demand_order(planes):
-    order, known = [], {(0, x) for x in range(planes)}
+    order, known = [], {(1, x) for x in range(planes)}
 
     def need(step, x):
         if (step, x) in known:
@@ -229,46 +229,31 @@
     onsite_ref[...] = onsite
     onsite_in[0] = onsite
 
-    order = demand_order(planes)
-    sequence = []
-    for step, x in order:
-        if step == 1:
-            wanted = [("plane", (x + near) % planes) for near in (-1, 0, 1)] + [("onsite", x)]
-            sequence += [item for item in wanted if item[1] and item not in sequence]
-    arriving = {}
     pl.semaphore_wait(barrier, cells * peers - 1)
-    for kind, slot in sequence:
-        hop = planes - slot
-        peer = lax.rem(place + hop, cells)
-        if kind == "plane":
-            copy = remote(
-                packed.at[peer], planes_in.at[slot], s1.at[hop], r1.at[hop], {"cells": peer}
-            )
-        else:
-            copy = remote(onsite_ref, onsite_in.at[slot], s6.at[hop], r6.at[hop], {"cells": peer})
-        copy.start()
-        arriving[kind, slot] = copy
-    sent = list(arriving.values())
+    plane_copies, onsite_copies = [], []
+    for hop in range(1, cells):
+        peer, slot = lax.rem(place + hop, cells), cells - hop
+        plane_copies.append(
+            remote(packed.at[peer], planes_in.at[slot], s1.at[hop], r1.at[hop], {"cells": peer})
+        )
+        onsite_copies.append(
+            remote(onsite_ref, onsite_in.at[slot], s6.at[hop], r6.at[hop], {"cells": peer})
+        )
+    for each in plane_copies + onsite_copies:
+        each.start()
     loads[2].wait()
     build_weights(hopping_ref, weights)
+    for each in plane_copies:
+        each.wait()
 
     def put(slot, x, value):
         fields[slot, x] = value
         high, low = split_pair(value)
         highs[slot, x], lows[slot, x] = high, low
 
-    ready = set()
-
-    def receive(x):
-        if x in ready:
-            return
-        ready.add(x)
-        if x:
-            arriving["plane", x].wait_recv()
-            pieces = [planes_in[x, t * orbits : (t + 1) * orbits, :] for t in range(own)]
-        else:
-            pieces = [packed[place, t * orbits : (t + 1) * orbits, :] for t in range(own)]
-        put(0, x, jnp.concatenate(pieces, axis=1))
+    for x in range(planes):
+        held = packed.at[place] if x == 0 else planes_in.at[x]
+        put(0, x, jnp.concatenate([held[t * orbits : (t + 1) * orbits, :] for t in range(own)], axis=1))
 
     def advance(step, x):
         now, later = (step - 1) % 2, step % 2
@@ -276,23 +261,25 @@
         high, low = [highs[now, r] for r in around], [lows[now, r] for r in around]
         source = jnp.concatenate(high + low + high, axis=0)
         product = jnp.dot(weights[...], source, preferred_element_type=jnp.float32)
-        onsite = onsite_in[x]
-        results = []
-        for t in range(own):
-            span = slice(t * lanes, (t + 1) * lanes)
-            applied = gather_shifts(product[:, span], orbits) + onsite * fields[now, x, :, span]
-            if step > 1:
-                applied = 2.0 * applied - fields[later, x, :, span]
-            results.append(applied)
-        return results
+        moved = [gather_shifts(product[:, t * lanes : (t + 1) * lanes], orbits) for t in range(own)]
+        if step == 1:
+            return moved
+        return [
+            2.0 * (each + onsite_in[x] * fields[now, x, :, span]) - fields[later, x, :, span]
+            for each, span in zip(moved, spans)
+        ]
+
+    spans = [slice(t * lanes, (t + 1) * lanes) for t in range(own)]
+    for x in range(planes):
+        fields[1, x] = jnp.concatenate(advance(1, x), axis=1)
+    for each in onsite_copies:
+        each.wait()
+    for x in range(planes):
+        onsite = jnp.concatenate([onsite_in[x]] * own, axis=1)
+        put(1, x, fields[1, x] + onsite * fields[0, x])
 
     copies = []
-    for step, x in order:
-        if step == 1:
-            for near in (-1, 0, 1):
-                receive((x + near) % planes)
-            if x:
-                arriving["onsite", x].wait_recv()
+    for step, x in demand_order(planes):
         results = advance(step, x)
         if step < STEPS:
             put(step % 2, x, jnp.concatenate(results, axis=1))
@@ -313,8 +300,6 @@
             copy.start()
             copies.append(copy)
     by_rows[me] = leaving[0, mine]
-    for each in sent:
-        each.wait_send()
     for each in copies:
         each.wait()
 

time: 65.6 us -> 60.3 us (0.919)
  Pallas kernels: 62.4 us -> 57.6 us
    pallas_call x1, Pallas kernels: 62.4 us -> 57.6 us  [resident_shards(): pl.pallas_call(functools.partial(whole_kernel, cells, peers, math.sqrt(fl...]
where the time goes in v4:
time: 60.3 us; the launch traced here: 60.1 us
  Pallas kernels  57.6 us (96%)
  local copies, waits for them, and re-layouts  1.87 us (3%)
  between operations  0.66 us (1%)
    pallas_call x1, Pallas kernels, resident_shards(): pl.pallas_call(functools.partial(whole_kernel, cells, peers, math.sqrt(fl...  57.6 us
    unnamed x1, local copies, waits for them, and re-layouts  1.87 us

profile of v4, /device:TPU:0, one launch (start us, length us, event | category | flops | bytes accessed | tf_op | source)
XLA Modules:
  0.0 60.1 jit_solution(1906954393386134978)
XLA Ops:
  0.7 57.6 %whole.1 = f32[4,16,16,128]{3,2,1,0:T(8,128)} custom-call(f32[1]{0:T(128)S(6)} %copy.7.center_ref, f32[1024,128]{1,0:T(8,128)} %bitcast.5, f32[64,1,128]{2,1,0:T(1,128)} %potential_any.1, f32[27,64,64]{2,1,0:T(8,128)} %hopping_any.1), custom_call_target="tpu_custom_call" | custom-call | tf_op jit(solution)/shard_map/whole/pallas_call | solution.py:358
  58.2 1.9 %copy.8 = f32[64,1,16,128]{3,2,1,0:T(8,128)} copy(f32[64,1,16,128]{3,2,1,0:T(8,128)} %bitcast.4) | data formatting | bytes 1048576

commit v5 on v4

--- a/solution.py
+++ b/solution.py
@@ -287,7 +287,7 @@
         for t in range(own):
             for p in range(peers):
                 leaving[x, p, t * rows : (t + 1) * rows, :] = results[t][p * rows : (p + 1) * rows]
-        for turn in range(1, peers) if x == 0 else range(peers):
+        for turn in list(range(1, peers)) + ([0] if x else []):
             p = lax.rem(mine + turn, peers)
             sem = x * peers + turn
             copy = remote(

time: 60.3 us -> 60.3 us (level)
  no operation moved by 1% of the time
where the time goes in v5:
time: 60.3 us; the launch traced here: 60.1 us
  Pallas kernels  57.6 us (96%)
  local copies, waits for them, and re-layouts  1.87 us (3%)
  between operations  0.66 us (1%)
    pallas_call x1, Pallas kernels, resident_shards(): pl.pallas_call(functools.partial(whole_kernel, cells, peers, math.sqrt(fl...  57.6 us
    unnamed x1, local copies, waits for them, and re-layouts  1.87 us

profile of v5, /device:TPU:0, one launch (start us, length us, event | category | flops | bytes accessed | tf_op | source)
XLA Modules:
  0.0 60.1 jit_solution(11304759573035713780)
XLA Ops:
  0.7 57.6 %whole.1 = f32[4,16,16,128]{3,2,1,0:T(8,128)} custom-call(f32[1]{0:T(128)S(6)} %copy.7.center_ref, f32[1024,128]{1,0:T(8,128)} %bitcast.5, f32[64,1,128]{2,1,0:T(1,128)} %potential_any.1, f32[27,64,64]{2,1,0:T(8,128)} %hopping_any.1), custom_call_target="tpu_custom_call" | custom-call | tf_op jit(solution)/shard_map/whole/pallas_call | solution.py:358
  58.2 1.9 %copy.8 = f32[64,1,16,128]{3,2,1,0:T(8,128)} copy(f32[64,1,16,128]{3,2,1,0:T(8,128)} %bitcast.4) | data formatting | bytes 1048576
